TPU v7x, 32 devices: a whole 2x2x4 slice. The times are simulated.
32 devices in a mesh: dp: 4 (over y, x), seq: 8 (over z, core).
Axes of the slice: x: 2, y: 2, z: 4, core: 2. Of those that a mesh axis runs over, the one named last changes fastest.
Arguments:
- tokens: bfloat16 [4, 16, 16, 4, 512], P('dp', 'seq'), may hold values from -6 to 6
- conv_first: bfloat16 [27, 512, 128], replicated, may hold values from -0.0546875 to 0.0546875
- bias_first: float32 [128], replicated, may hold values from -3 to 3
- conv_second: bfloat16 [27, 128, 384], replicated, may hold values from -0.109375 to 0.109375
- bias_second: float32 [384], replicated, may hold values from -3 to 3
- pixels: bfloat16 [4, 16, 16, 4, 1536], P('dp', None, 'seq'), may hold values from 0 to 1
- mask_index: int32 [4, 57], P('dp'), may hold values from 0 to 63, as said below
Outputs:
- grad_first: float32 [27, 512, 128], P(None, 'seq', 'dp')
- grad_second: float32 [27, 128, 384], P(None, 'seq', 'dp')
Inputs may be any that keep to these rules, and one draw needn't show every extreme that they name: `mask_index`: each row holds 57 distinct positions of the 16 x 4 token grid.
All inputs are finite; a program needn't handle non-finite values.
Results may differ from a plain program's by a relative error of at most 0.003.
Values may be sent and summed in bfloat16 or wider, within the bound.
A program may use at most 128 MiB of HBM per device.

v0:
```python
import jax
import jax.numpy as jnp
from jax import lax
from jax.experimental import pallas as pl
from jax.experimental.pallas import tpu as pltpu
from jax.sharding import PartitionSpec as P

F32 = jnp.float32
BF16 = jnp.bfloat16
NT = (((1,), (1,)), ((), ()))
GELU_ROOT = 0.7978845608028654
GELU_CUBE = 0.044715


def floor_half(v):
    return v // 2 if v >= 0 else -1


def make_kernel(dims):
    ndp, nseq, frames, tf, rows, cols, width, mid, values = dims
    n = tf * cols * rows
    plane = cols * rows
    dblk = width // nseq
    cblk = mid // ndp
    vblk = values // ndp
    mblk = mid // nseq
    ndev = ndp * nseq
    clip_lanes = nseq * n

    def kernel(tok, w1_hbm, b1, w2_hbm, b2, pix, perm, colv, lanev, lanes_n, o1, o2,
               w1, w2, xbuf, xall, thalo, pxall, tfield, im1, hsend, hhalo, hfield, im2,
               psend, phalo, csend, call_, htsend, htall, rsend, rall, gsend, gall, acc,
               wsem, th_s, th_r, px_s, px_r, x_s, x_r, hh_s, hh_r, ph_s, ph_r,
               c_s, c_r, ht_s, ht_r, r_s, r_r, g_s, g_r):
        dp = lax.axis_index("dp")
        seq = lax.axis_index("seq")
        me = dp * nseq + seq
        nxt = lax.rem(seq + 1, nseq)
        prv = lax.rem(seq + nseq - 1, nseq)

        def remote(src, dst, ss, rs, d, s):
            return pltpu.make_async_remote_copy(
                src_ref=src, dst_ref=dst, send_sem=ss, recv_sem=rs,
                device_id=(d, s), device_id_type=pl.DeviceIdType.MESH)

        cp1 = pltpu.make_async_copy(w1_hbm, w1, wsem.at[0])
        cp2 = pltpu.make_async_copy(w2_hbm, w2, wsem.at[1])
        cp1.start()
        cp2.start()

        barrier = pltpu.get_barrier_semaphore()

        def greet(o, c):
            t = lax.rem(me + o, ndev)
            pl.semaphore_signal(barrier, inc=1, device_id=(t // nseq, lax.rem(t, nseq)),
                                device_id_type=pl.DeviceIdType.MESH)
            return c

        lax.fori_loop(1, ndev, greet, 0)

        flat = tok[...].reshape(n, width).astype(F32)
        xt = flat.T
        for s in range(nseq):
            xbuf[s] = xt[s * dblk:(s + 1) * dblk].astype(BF16)
        pl.semaphore_wait(barrier, ndev - 1)

        def halo(first, last, dst, ss, rs):
            return (remote(last, dst.at[0], ss.at[0], rs.at[0], dp, nxt),
                    remote(first, dst.at[1], ss.at[1], rs.at[1], dp, prv))

        th = halo(tok.at[0], tok.at[tf - 1], thalo, th_s, th_r)
        for c in th:
            c.start()

        def px_copy(o):
            s = lax.rem(seq + o, nseq)
            return remote(pix.at[s], pxall.at[seq], px_s.at[o], px_r.at[seq], dp, s)

        def px_arrival(o):
            s = lax.rem(seq + nseq - o, nseq)
            return remote(pix.at[s], pxall.at[s], px_s.at[o], px_r.at[s], dp, s)

        def x_copy(o):
            t = lax.rem(me + o, ndev)
            s = lax.rem(t, nseq)
            return remote(xbuf.at[s], xall.at[me], x_s.at[o], x_r.at[me], t // nseq, s)

        def x_arrival(o):
            t = lax.rem(me + ndev - o, ndev)
            s = lax.rem(t, nseq)
            return remote(xbuf.at[s], xall.at[t], x_s.at[o], x_r.at[t], t // nseq, s)

        def c_pair(o):
            d = lax.rem(dp + o, ndp)
            return (remote(csend.at[d], call_.at[dp], c_s.at[o], c_r.at[dp], d, seq),
                    remote(htsend, htall.at[dp], ht_s.at[o], ht_r.at[dp], d, seq))

        def c_arrival(o):
            d = lax.rem(dp + ndp - o, ndp)
            return (remote(csend.at[d], call_.at[d], c_s.at[o], c_r.at[d], d, seq),
                    remote(htsend, htall.at[d], ht_s.at[o], ht_r.at[d], d, seq))

        def r_copy(o):
            s = lax.rem(seq + o, nseq)
            return remote(rsend.at[s], rall.at[seq], r_s.at[o], r_r.at[seq], dp, s)

        def r_arrival(o):
            s = lax.rem(seq + nseq - o, nseq)
            return remote(rsend.at[s], rall.at[s], r_s.at[o], r_r.at[s], dp, s)

        def g_copy(o):
            t = lax.rem(me + o, ndev)
            d = t // nseq
            return remote(gsend.at[d], gall.at[me], g_s.at[o], g_r.at[me], d, lax.rem(t, nseq))

        def g_arrival(o):
            t = lax.rem(me + ndev - o, ndev)
            d = t // nseq
            return remote(gsend.at[d], gall.at[t], g_s.at[o], g_r.at[t], d, lax.rem(t, nseq))

        def each(count, act):
            def body(o, c):
                act(o)
                return c
            lax.fori_loop(1, count, body, 0)

        def start_all(count, copy):
            each(count, lambda o: copy(o).start())

        def finish(count, copy, arrival):
            each(count, lambda o: copy(o).wait_send())
            each(count, lambda o: arrival(o).wait_recv())

        start_all(nseq, px_copy)
        start_all(ndev, x_copy)
        xall[me] = xbuf[seq]
        pxall[seq] = pix[seq]

        scale = colv[:, 0:1]
        h_low, h_high = colv[:, 1:2], colv[:, 2:3]
        w_low, w_high = colv[:, 3:4], colv[:, 4:5]

        def row_shift(v, d):
            m = v.shape[0]
            if d == 0:
                return v
            rolled = pltpu.roll(v, 1 if d < 0 else m - 1, axis=0)
            return rolled * (h_low if d < 0 else h_high)[:m]

        def col_shift(v, d):
            m = v.shape[0]
            if d == 0:
                return v
            rolled = pltpu.roll(v, rows if d < 0 else m - rows, axis=0)
            return rolled * (w_low if d < 0 else w_high)[:m]

        def place(field, frame, v, count):
            for d in (-1, 0, 1):
                field[d + 1, frame:frame + count, 1:cols + 1] = (
                    row_shift(v, d).astype(BF16).reshape(count, cols, rows, v.shape[1]))

        def edges(field):
            zero = jnp.zeros((3, tf + 2, 1, rows, field.shape[4]), BF16)
            field[:, :, 0:1] = zero
            field[:, :, cols + 1:cols + 2] = zero

        first = jnp.where(seq > 0, 1.0, 0.0).astype(F32)
        final = jnp.where(seq < nseq - 1, 1.0, 0.0).astype(F32)

        edges(tfield)
        edges(hfield)
        place(tfield, 1, flat, tf)
        for c in th:
            c.wait()
        place(tfield, 0, thalo[0].reshape(plane, width).astype(F32) * first, 1)
        place(tfield, tf + 1, thalo[1].reshape(plane, width).astype(F32) * final, 1)
        for k in range(27):
            a, b, c = k // 9, k // 3 % 3, k % 3
            im1[:, k * width:(k + 1) * width] = (
                tfield[b, a:a + tf, c:c + cols].reshape(n, width))
        cp1.wait()
        z = jnp.dot(im1[...], w1[...], preferred_element_type=F32) + b1[...]
        th_ = jnp.tanh(GELU_ROOT * (z + GELU_CUBE * z * z * z))
        slope = 0.5 * (1.0 + th_) + 0.5 * z * (1.0 - th_ * th_) * GELU_ROOT * (
            1.0 + 3.0 * GELU_CUBE * z * z)
        hid = (0.5 * z * (1.0 + th_)).astype(BF16)
        hsend[...] = hid.reshape(tf, cols, rows, mid)
        hh = halo(hsend.at[0], hsend.at[tf - 1], hhalo, hh_s, hh_r)
        for c in hh:
            c.start()
        hid_f = hid.astype(F32)
        place(hfield, 1, hid_f, tf)

        finish(nseq, px_copy, px_arrival)
        pix_rows = pxall[...].astype(F32).reshape(n, 4 * values).astype(BF16)
        px = jnp.dot(perm[...], pix_rows, preferred_element_type=F32)
        center = px - jnp.mean(px, axis=-1, keepdims=True)
        spread = jnp.mean(center * center, axis=-1, keepdims=True)
        normed = center * lax.rsqrt(spread + 1e-06)

        for c in hh:
            c.wait()
        before = hhalo[0].reshape(plane, mid).astype(F32) * first
        after = hhalo[1].reshape(plane, mid).astype(F32) * final
        place(hfield, 0, before, 1)
        place(hfield, tf + 1, after, 1)

        for ij in range(4):
            i, j = ij // 2, ij % 2
            for k in range(27):
                a, b, c = k // 9, k // 3 % 3, k % 3
                dh, dw = floor_half(i + b - 1), floor_half(j + c - 1)
                im2[ij * n:(ij + 1) * n, k * mid:(k + 1) * mid] = (
                    hfield[dh + 1, a:a + tf, dw + 1:dw + 1 + cols].reshape(n, mid))
        cp2.wait()
        predict = jnp.dot(im2[...], w2[...], preferred_element_type=F32) + b2[...]
        cots = []
        for ij in range(4):
            cot = (scale * (predict[ij * n:(ij + 1) * n]
                            - normed[:, ij * values:(ij + 1) * values])).astype(BF16).astype(F32)
            cots.append(cot)
            turned = cot.T
            for d in range(ndp):
                csend[d, ij] = turned[d * vblk:(d + 1) * vblk].astype(BF16)
        time_line = jnp.concatenate([before, hid_f, after], axis=0)
        for a in range(3):
            htsend[a * mid:(a + 1) * mid] = (
                time_line[a * plane:a * plane + n].T.astype(BF16))
        each(ndp, lambda o: [c.start() for c in c_pair(o)])
        call_[dp] = csend[dp]
        htall[dp] = htsend[...]

        def pair_sums(low, high, shift):
            return (high + shift(low, 1), low + high, shift(high, -1) + low)

        def cell_sums(parts, rshift, cshift):
            by_col = [pair_sums(parts[j], parts[2 + j], rshift) for j in range(2)]
            return [s for b in range(3)
                    for s in pair_sums(by_col[0][b], by_col[1][b], cshift)]

        sums = [s.astype(BF16) for s in cell_sums(cots, row_shift, col_shift)]
        backs = []
        for a in range(3):
            total = jnp.zeros((n, mid), F32)
            for bc in range(9):
                k = a * 9 + bc
                total = total + lax.dot_general(
                    sums[bc], w2[k * mid:(k + 1) * mid], NT, preferred_element_type=F32)
            backs.append(total)
        psend[0] = backs[2][n - plane:]
        psend[1] = backs[0][:plane]
        ph = halo(psend.at[1], psend.at[0], phalo, ph_s, ph_r)
        for c in ph:
            c.start()
        for c in ph:
            c.wait()
        from_prev, from_next = phalo[0] * first, phalo[1] * final
        if tf > 1:
            late = jnp.concatenate([from_prev, backs[2][:n - plane]], axis=0)
            early = jnp.concatenate([backs[0][plane:], from_next], axis=0)
        else:
            late, early = from_prev, from_next
        grad_z = ((backs[1] + late + early) * slope).astype(BF16).astype(F32).T
        for d in range(ndp):
            gsend[d] = grad_z[d * cblk:(d + 1) * cblk].astype(BF16)
        start_all(ndev, g_copy)
        gall[me] = gsend[dp]

        each(ndp, lambda o: [c.wait_send() for c in c_pair(o)])
        each(ndp, lambda o: [c.wait_recv() for c in c_arrival(o)])

        def lane_row(v, d):
            rolled = pltpu.roll(v, 1 if d < 0 else n - 1, axis=1)
            return rolled * (lanes_n[0:1] if d < 0 else lanes_n[1:2])

        def lane_col(v, d):
            rolled = pltpu.roll(v, rows if d < 0 else n - rows, axis=1)
            return rolled * (lanes_n[2:3] if d < 0 else lanes_n[3:4])

        acc[...] = jnp.zeros_like(acc)

        def one_clip(q, carry):
            parts = [call_[q, ij].astype(F32) for ij in range(4)]
            stack = jnp.concatenate(cell_sums(parts, lane_row, lane_col), axis=0).astype(BF16)
            acc[...] += lax.dot_general(htall[q], stack, NT, preferred_element_type=F32)
            return carry

        lax.fori_loop(0, ndp, one_clip, 0)
        for s in range(nseq):
            for a in range(3):
                lo = a * mid + s * mblk
                rsend[s, a] = acc[lo:lo + mblk].astype(BF16)
        start_all(nseq, r_copy)
        rall[seq] = rsend[seq]

        finish(ndev, x_copy, x_arrival)
        finish(ndev, g_copy, g_arrival)
        o1[...] = jnp.zeros_like(o1)

        def one_first(q, carry):
            base = q * nseq
            g = jnp.concatenate([gall[base + s].astype(F32) for s in range(nseq)], axis=1)
            x = jnp.concatenate([xall[base + s] for s in range(nseq)], axis=1)
            pieces = []
            by_row = []
            for b in range(3):
                d = b - 1
                if d == 0:
                    by_row.append(g)
                else:
                    m = pltpu.roll(g, d % clip_lanes, axis=1)
                    by_row.append(m * (lanev[0:1] if d > 0 else lanev[1:2]))
            grid = {}
            for b in range(3):
                for c in range(3):
                    d = c - 1
                    v = by_row[b]
                    if d != 0:
                        v = pltpu.roll(v, (d * rows) % clip_lanes, axis=1)
                        v = v * (lanev[2:3] if d > 0 else lanev[3:4])
                    grid[b, c] = v
            for a in range(3):
                for b in range(3):
                    for c in range(3):
                        d = a - 1
                        v = grid[b, c]
                        if d != 0:
                            v = pltpu.roll(v, (d * plane) % clip_lanes, axis=1)
                            v = v * (lanev[4:5] if d > 0 else lanev[5:6])
                        pieces.append(v)
            stack = jnp.concatenate(pieces, axis=0).astype(BF16)
            o1[...] += lax.dot_general(stack, x, NT, preferred_element_type=F32)
            return carry

        lax.fori_loop(0, ndp, one_first, 0)

        finish(nseq, r_copy, r_arrival)
        total = rall[0].astype(F32)
        for s in range(1, nseq):
            total = total + rall[s].astype(F32)
        o2[...] = total

    return kernel


def per_device(tokens, conv_first, bias_first, conv_second, bias_second, pixels, mask_index):
    ndp, nseq = lax.axis_size("dp"), lax.axis_size("seq")
    tf, rows, cols, width = tokens.shape[1:]
    frames = tf * nseq
    mid, values = conv_second.shape[1], conv_second.shape[2]
    n = tf * rows * cols
    hb = rows // nseq
    dims = (ndp, nseq, frames, tf, rows, cols, width, mid, values)
    plane = rows * cols
    dblk, cblk, vblk, mblk = width // nseq, mid // ndp, values // ndp, mid // nseq
    ndev = ndp * nseq

    tok = tokens[0].transpose(0, 2, 1, 3)
    pix = pixels[0].reshape(nseq, tf * hb * cols, 4 * values)
    idx = jnp.arange(n, dtype=jnp.int32)
    t_of, w_of, h_of = idx // plane, idx // rows % cols, idx % rows
    source = (h_of // hb) * (tf * hb * cols) + t_of * (hb * cols) + (h_of % hb) * cols + w_of
    perm = (source[:, None] == idx[None, :]).astype(BF16)
    position = h_of * cols + w_of
    hits = jnp.sum((position[:, None] == mask_index[0][None, :]).astype(F32), axis=1)
    colv = jnp.stack([2.0 / (4 * values) * hits, h_of > 0, h_of < rows - 1,
                      w_of > 0, w_of < cols - 1], axis=1).astype(F32)
    lanes_n = jnp.stack([h_of > 0, h_of < rows - 1, w_of > 0, w_of < cols - 1]).astype(F32)
    lid = jnp.arange(frames * plane, dtype=jnp.int32)
    tl, wl, hl = lid // plane, lid // rows % cols, lid % rows
    lanev = jnp.stack([hl > 0, hl < rows - 1, wl > 0, wl < cols - 1,
                       tl > 0, tl < frames - 1]).astype(F32)

    vm = pl.BlockSpec(memory_space=pltpu.VMEM)
    hbm = pl.BlockSpec(memory_space=pl.ANY)

    def dma(k):
        return pltpu.SemaphoreType.DMA((k,))

    scratch = [
        pltpu.VMEM((27 * width, mid), BF16),
        pltpu.VMEM((27 * mid, values), BF16),
        pltpu.VMEM((nseq, dblk, n), BF16),
        pltpu.VMEM((ndev, dblk, n), BF16),
        pltpu.VMEM((2, cols, rows, width), BF16),
        pltpu.VMEM(pix.shape, BF16),
        pltpu.VMEM((3, tf + 2, cols + 2, rows, width), BF16),
        pltpu.VMEM((n, 27 * width), BF16),
        pltpu.VMEM((tf, cols, rows, mid), BF16),
        pltpu.VMEM((2, cols, rows, mid), BF16),
        pltpu.VMEM((3, tf + 2, cols + 2, rows, mid), BF16),
        pltpu.VMEM((4 * n, 27 * mid), BF16),
        pltpu.VMEM((2, plane, mid), F32),
        pltpu.VMEM((2, plane, mid), F32),
        pltpu.VMEM((ndp, 4, vblk, n), BF16),
        pltpu.VMEM((ndp, 4, vblk, n), BF16),
        pltpu.VMEM((3 * mid, n), BF16),
        pltpu.VMEM((ndp, 3 * mid, n), BF16),
        pltpu.VMEM((nseq, 3, mblk, 9 * vblk), BF16),
        pltpu.VMEM((nseq, 3, mblk, 9 * vblk), BF16),
        pltpu.VMEM((ndp, cblk, n), BF16),
        pltpu.VMEM((ndev, cblk, n), BF16),
        pltpu.VMEM((3 * mid, 9 * vblk), F32),
        dma(2), dma(2), dma(2), dma(nseq), dma(nseq), dma(ndev), dma(ndev),
        dma(2), dma(2), dma(2), dma(2), dma(ndp), dma(ndp), dma(ndp), dma(ndp),
        dma(nseq), dma(nseq), dma(ndev), dma(ndev),
    ]
    first, second = pl.pallas_call(
        make_kernel(dims),
        out_shape=(jax.ShapeDtypeStruct((27 * cblk, dblk), F32),
                   jax.ShapeDtypeStruct((3, mblk, 9 * vblk), F32)),
        in_specs=[vm, hbm, vm, hbm, vm, vm, vm, vm, vm, vm],
        out_specs=(vm, vm),
        scratch_shapes=scratch,
        compiler_params=pltpu.CompilerParams(
            collective_id=0, has_side_effects=True, vmem_limit_bytes=60 * 1024 * 1024),
        name="step",
    )(tok, conv_first.reshape(27 * width, mid), bias_first.reshape(1, mid),
      conv_second.reshape(27 * mid, values), bias_second.reshape(1, values),
      pix, perm, colv, lanev, lanes_n)
    first = first.reshape(27, cblk, dblk).transpose(0, 2, 1)
    second = second.reshape(3, mblk, 9, vblk).transpose(0, 2, 1, 3).reshape(27, mblk, vblk)
    return (first, second)


def solution(mesh):
    return jax.shard_map(
        per_device,
        mesh=mesh,
        in_specs=(
            P("dp", "seq", None, None, None),
            P(),
            P(),
            P(),
            P(),
            P("dp", None, "seq", None, None),
            P("dp", None),
        ),
        out_specs=(P(None, "seq", "dp"), P(None, "seq", "dp")),
        check_vma=False,
    )
```

profile of v0, /device:TPU:9, one launch (start us, length us, event | category | flops | bytes accessed | tf_op | source)
XLA Modules:
  0.0 69.6 jit_solution(7306571092590356382)
XLA Ops:
  0.6 0.7 %convert_reduce_fusion = f32[128]{0:T(128)S(1)} fusion(s32[128]{0:T(128)S(1)} %multiply_add_fusion, s32[57]{0:T(128)} %bitcast.23), kind=kLoop, calls=%fused_computation.3 | loop fusion | flops 21760 | bytes 1252 | tf_op jit(solution)/shard_map/reduce_sum | solution.py:365
  1.4 0.6 add_convert_fusion.lanes_n
  2.1 1.2 %reshape.418.b2 = f32[1,384]{1,0:T(1,128)} reshape(f32[384]{0:T(512)} %param.11) | data formatting | bytes 3072 | tf_op jit(solution)/shard_map/reshape | solution.py:419
  3.4 0.1 stack.7
  3.5 0.6 convert_element_type.58.lanev
  4.1 0.7 fusion.perm
  4.7 0.7 %copy.21.colv = f32[128,5]{1,0:T(8,128)} copy(f32[128,5]{0,1:T(8,128)S(1)} %stack.6) | data formatting | bytes 5120 | tf_op jit(solution)/shard_map/stack | solution.py:366
  5.5 1.6 %copy.24 = bf16[1,2,16,4,512]{4,2,3,1,0:T(8,128)(2,1)} copy(bf16[1,2,16,4,512]{4,3,2,1,0:T(4,128)(2,1)} %param.7) | data formatting | bytes 262144 | tf_op args[0]
  7.1 1.8 %reshape_squeeze.3.pix = bf16[8,16,1536]{2,1,0:T(8,128)(2,1)} reshape(bf16[1,16,2,4,1536]{4,3,2,1,0:T(4,128)(2,1)} %param.12) | data formatting | bytes 786432 | tf_op jit(solution)/shard_map/reshape;squeeze | solution.py:359
  8.9 57.1 %step.1 = (f32[864,64]{1,0:T(8,128)}, f32[3,16,864]{2,1,0:T(8,128)}) custom-call(bf16[2,4,16,512]{3,2,1,0:T(8,128)(2,1)} %bitcast.19, bf16[13824,128]{1,0:T(8,128)(2,1)} %bitcast.16, f32[1,128]{1,0:T(1,128)} %bitcast.22, bf16[3456,384]{1,0:T(8,128)(2,1)} %bitcast.17, f32[1,384]{1,0:T(1,128)} %reshape.418.b2, bf16[8,16,1536]{2,1,0:T(8,128)(2,1)} %reshape_squeeze.3.pix, ...), custom_call_target="tpu_custom_call" | custom-call | tf_op jit(solution)/shard_map/step/pallas_call | solution.py:408
  66.0 1.1 %reshape.420 = f32[3,16,9,96]{3,2,1,0:T(8,128)S(1)} reshape(f32[3,16,864]{2,1,0:T(8,128)} %get-tuple-element.5) | data formatting | bytes 331776 | tf_op jit(solution)/shard_map/reshape | solution.py:422
  67.0 0.8 %copy.22 = f32[3,9,16,96]{3,2,1,0:T(8,128)} copy(f32[3,9,16,96]{3,1,2,0:T(8,128)S(1)} %bitcast.18) | data formatting | bytes 331776 | tf_op jit(solution)/shard_map/transpose | solution.py:422
  67.8 1.8 %copy.26 = f32[27,64,32]{1,2,0:T(8,128)} copy(f32[27,64,32]{1,2,0:T(8,128)} %bitcast.20) | data formatting | bytes 442368
  (11 shorter events, 0.1 us)
where the time goes:
time: 69.9 us; the launch traced here: 69.6 us
  Pallas kernels  57.1 us (82%)
  local copies, waits for them, and re-layouts  9.08 us (13%)
  other arithmetic  2.75 us (4%)
    pallas_call x1, Pallas kernels, per_device(): pl.pallas_call(make_kernel(dims), out_shape=(jax.ShapeDtypeStruct((27 * c...  57.1 us
    unnamed x2, local copies, waits for them, and re-layouts  3.39 us
    another operation x1, local copies, waits for them, and re-layouts, per_device(): pix = pixels[0].reshape(nseq, tf * hb * cols, 4 * values)  1.83 us

commit v1 on v0

--- a/solution.py
+++ b/solution.py
@@ -1,5 +1,6 @@
 import jax
 import jax.numpy as jnp
+import numpy as np
 from jax import lax
 from jax.experimental import pallas as pl
 from jax.experimental.pallas import tpu as pltpu
@@ -27,7 +28,8 @@
     ndev = ndp * nseq
     clip_lanes = nseq * n
 
-    def kernel(tok, w1_hbm, b1, w2_hbm, b2, pix, perm, colv, lanev, lanes_n, o1, o2,
+    def kernel(tok, w1_hbm, b1, w2_hbm, b2, pix, marks, place_of, tperm, perm, colv, lanev,
+               lanes_n, o1, o2,
                w1, w2, xbuf, xall, thalo, pxall, tfield, im1, hsend, hhalo, hfield, im2,
                psend, phalo, csend, call_, htsend, htall, rsend, rall, gsend, gall, acc,
                wsem, th_s, th_r, px_s, px_r, x_s, x_r, hh_s, hh_r, ph_s, ph_r,
@@ -58,7 +60,11 @@
 
         lax.fori_loop(1, ndev, greet, 0)
 
-        flat = tok[...].reshape(n, width).astype(F32)
+        def ordered(frame):
+            raw = frame.astype(F32).reshape(plane, width).astype(BF16)
+            return jnp.dot(tperm[...], raw, preferred_element_type=F32)
+
+        flat = jnp.concatenate([ordered(tok[t]) for t in range(tf)], axis=0)
         xt = flat.T
         for s in range(nseq):
             xbuf[s] = xt[s * dblk:(s + 1) * dblk].astype(BF16)
@@ -74,11 +80,12 @@
 
         def px_copy(o):
             s = lax.rem(seq + o, nseq)
-            return remote(pix.at[s], pxall.at[seq], px_s.at[o], px_r.at[seq], dp, s)
+            return remote(pix.at[pl.ds(s * tf, tf)], pxall.at[seq], px_s.at[o], px_r.at[seq],
+                          dp, s)
 
         def px_arrival(o):
             s = lax.rem(seq + nseq - o, nseq)
-            return remote(pix.at[s], pxall.at[s], px_s.at[o], px_r.at[s], dp, s)
+            return remote(pix.at[pl.ds(s * tf, tf)], pxall.at[s], px_s.at[o], px_r.at[s], dp, s)
 
         def x_copy(o):
             t = lax.rem(me + o, ndev)
@@ -134,9 +141,11 @@
         start_all(nseq, px_copy)
         start_all(ndev, x_copy)
         xall[me] = xbuf[seq]
-        pxall[seq] = pix[seq]
-
-        scale = colv[:, 0:1]
+        own = pltpu.make_async_copy(pix.at[pl.ds(seq * tf, tf)], pxall.at[seq], wsem.at[2])
+        own.start()
+
+        matches = (place_of[...] == marks[...]).astype(F32)
+        scale = 2.0 / (4 * values) * jnp.sum(matches, axis=1, keepdims=True)
         h_low, h_high = colv[:, 1:2], colv[:, 2:3]
         w_low, w_high = colv[:, 3:4], colv[:, 4:5]
 
@@ -172,8 +181,8 @@
         place(tfield, 1, flat, tf)
         for c in th:
             c.wait()
-        place(tfield, 0, thalo[0].reshape(plane, width).astype(F32) * first, 1)
-        place(tfield, tf + 1, thalo[1].reshape(plane, width).astype(F32) * final, 1)
+        place(tfield, 0, ordered(thalo[0]) * first, 1)
+        place(tfield, tf + 1, ordered(thalo[1]) * final, 1)
         for k in range(27):
             a, b, c = k // 9, k // 3 % 3, k % 3
             im1[:, k * width:(k + 1) * width] = (
@@ -191,6 +200,7 @@
         hid_f = hid.astype(F32)
         place(hfield, 1, hid_f, tf)
 
+        own.wait()
         finish(nseq, px_copy, px_arrival)
         pix_rows = pxall[...].astype(F32).reshape(n, 4 * values).astype(BF16)
         px = jnp.dot(perm[...], pix_rows, preferred_element_type=F32)
@@ -213,7 +223,7 @@
                 im2[ij * n:(ij + 1) * n, k * mid:(k + 1) * mid] = (
                     hfield[dh + 1, a:a + tf, dw + 1:dw + 1 + cols].reshape(n, mid))
         cp2.wait()
-        predict = jnp.dot(im2[...], w2[...], preferred_element_type=F32) + b2[...]
+        predict = jnp.dot(im2[...], w2[...], preferred_element_type=F32) + b2[...].reshape(1, values)
         cots = []
         for ij in range(4):
             cot = (scale * (predict[ij * n:(ij + 1) * n]
@@ -338,7 +348,9 @@
         total = rall[0].astype(F32)
         for s in range(1, nseq):
             total = total + rall[s].astype(F32)
-        o2[...] = total
+        for a in range(3):
+            for bc in range(9):
+                o2[a * 9 + bc] = total[a, :, bc * vblk:(bc + 1) * vblk]
 
     return kernel
 
@@ -355,21 +367,20 @@
     dblk, cblk, vblk, mblk = width // nseq, mid // ndp, values // ndp, mid // nseq
     ndev = ndp * nseq
 
-    tok = tokens[0].transpose(0, 2, 1, 3)
-    pix = pixels[0].reshape(nseq, tf * hb * cols, 4 * values)
-    idx = jnp.arange(n, dtype=jnp.int32)
+    idx = np.arange(n, dtype=np.int32)
     t_of, w_of, h_of = idx // plane, idx // rows % cols, idx % rows
     source = (h_of // hb) * (tf * hb * cols) + t_of * (hb * cols) + (h_of % hb) * cols + w_of
-    perm = (source[:, None] == idx[None, :]).astype(BF16)
-    position = h_of * cols + w_of
-    hits = jnp.sum((position[:, None] == mask_index[0][None, :]).astype(F32), axis=1)
-    colv = jnp.stack([2.0 / (4 * values) * hits, h_of > 0, h_of < rows - 1,
-                      w_of > 0, w_of < cols - 1], axis=1).astype(F32)
-    lanes_n = jnp.stack([h_of > 0, h_of < rows - 1, w_of > 0, w_of < cols - 1]).astype(F32)
-    lid = jnp.arange(frames * plane, dtype=jnp.int32)
+    perm = jnp.asarray(source[:, None] == idx[None, :], BF16)
+    flat_place = (h_of * cols + w_of)[:plane]
+    tperm = jnp.asarray(flat_place[:, None] == idx[None, :plane], BF16)
+    place_of = jnp.asarray((h_of * cols + w_of)[:, None])
+    colv = jnp.asarray(np.stack([h_of < 0, h_of > 0, h_of < rows - 1,
+                                 w_of > 0, w_of < cols - 1], axis=1), F32)
+    lanes_n = jnp.asarray(np.stack([h_of > 0, h_of < rows - 1, w_of > 0, w_of < cols - 1]), F32)
+    lid = np.arange(frames * plane, dtype=np.int32)
     tl, wl, hl = lid // plane, lid // rows % cols, lid % rows
-    lanev = jnp.stack([hl > 0, hl < rows - 1, wl > 0, wl < cols - 1,
-                       tl > 0, tl < frames - 1]).astype(F32)
+    lanev = jnp.asarray(np.stack([hl > 0, hl < rows - 1, wl > 0, wl < cols - 1,
+                                  tl > 0, tl < frames - 1]), F32)
 
     vm = pl.BlockSpec(memory_space=pltpu.VMEM)
     hbm = pl.BlockSpec(memory_space=pl.ANY)
@@ -382,8 +393,8 @@
         pltpu.VMEM((27 * mid, values), BF16),
         pltpu.VMEM((nseq, dblk, n), BF16),
         pltpu.VMEM((ndev, dblk, n), BF16),
-        pltpu.VMEM((2, cols, rows, width), BF16),
-        pltpu.VMEM(pix.shape, BF16),
+        pltpu.VMEM((2, rows, cols, width), BF16),
+        pltpu.VMEM((nseq, tf, hb, cols, 4 * values), BF16),
         pltpu.VMEM((3, tf + 2, cols + 2, rows, width), BF16),
         pltpu.VMEM((n, 27 * width), BF16),
         pltpu.VMEM((tf, cols, rows, mid), BF16),
@@ -401,25 +412,24 @@
         pltpu.VMEM((ndp, cblk, n), BF16),
         pltpu.VMEM((ndev, cblk, n), BF16),
         pltpu.VMEM((3 * mid, 9 * vblk), F32),
-        dma(2), dma(2), dma(2), dma(nseq), dma(nseq), dma(ndev), dma(ndev),
+        dma(3), dma(2), dma(2), dma(nseq), dma(nseq), dma(ndev), dma(ndev),
         dma(2), dma(2), dma(2), dma(2), dma(ndp), dma(ndp), dma(ndp), dma(ndp),
         dma(nseq), dma(nseq), dma(ndev), dma(ndev),
     ]
     first, second = pl.pallas_call(
         make_kernel(dims),
         out_shape=(jax.ShapeDtypeStruct((27 * cblk, dblk), F32),
-                   jax.ShapeDtypeStruct((3, mblk, 9 * vblk), F32)),
-        in_specs=[vm, hbm, vm, hbm, vm, vm, vm, vm, vm, vm],
+                   jax.ShapeDtypeStruct((27, mblk, vblk), F32)),
+        in_specs=[vm, hbm, vm, hbm, vm, hbm, vm, vm, vm, vm, vm, vm, vm],
         out_specs=(vm, vm),
         scratch_shapes=scratch,
         compiler_params=pltpu.CompilerParams(
             collective_id=0, has_side_effects=True, vmem_limit_bytes=60 * 1024 * 1024),
         name="step",
-    )(tok, conv_first.reshape(27 * width, mid), bias_first.reshape(1, mid),
-      conv_second.reshape(27 * mid, values), bias_second.reshape(1, values),
-      pix, perm, colv, lanev, lanes_n)
+    )(tokens[0], conv_first.reshape(27 * width, mid), bias_first.reshape(1, mid),
+      conv_second.reshape(27 * mid, values), bias_second,
+      pixels[0], mask_index, place_of, tperm, perm, colv, lanev, lanes_n)
     first = first.reshape(27, cblk, dblk).transpose(0, 2, 1)
-    second = second.reshape(3, mblk, 9, vblk).transpose(0, 2, 1, 3).reshape(27, mblk, vblk)
     return (first, second)
 
 

time: 69.9 us -> 61.4 us (0.88)
  local copies, waits for them, and re-layouts: 9.08 us -> 3.44 us
  other arithmetic: 2.75 us -> 0 us
    another operation x4 -> x0, local copies, waits for them, and re-layouts: 2.64 us -> none  [the longest x1 1.83 us: per_device(): pix = pixels[0].reshape(nseq, tf * hb * cols, 4 * values)]
    reshape x2 -> x0, local copies, waits for them, and re-layouts: 2.3 us -> none  [the longest x1 1.25 us: per_device(): bias_second.reshape(1, values)]
    convert_element_type x5 -> x0, other arithmetic: 1.9 us -> none  [the longest x1 0.68 us: per_device(): perm = (source[:, None] == idx[None, :]).astype(BF16)]
    transpose x1 -> x0, local copies, waits for them, and re-layouts: 0.76 us -> none  [per_device(): second.reshape(3, mblk, 9, vblk).transpose(0, 2, 1, 3)]
    reduce_sum x1 -> x0, other arithmetic: 0.75 us -> none  [per_device(): jnp.sum((position[:, None] == mask_index[0][None, :]).astype(F32), axis=1)]
where the time goes in v1:
time: 61.4 us; the launch traced here: 61.2 us
  Pallas kernels  57.1 us (93%)
  local copies, waits for them, and re-layouts  3.44 us (6%)
  between operations  0.64 us (1%)
    pallas_call x1, Pallas kernels, per_device(): pl.pallas_call(make_kernel(dims), out_shape=(jax.ShapeDtypeStruct((27 * c...  57.1 us
    unnamed x2, local copies, waits for them, and re-layouts  3.44 us

profile of v1, /device:TPU:9, one launch (start us, length us, event | category | flops | bytes accessed | tf_op | source)
XLA Modules:
  0.0 61.2 jit_solution(1680517112353748439)
XLA Ops:
  0.6 57.1 %step.1 = (f32[864,64]{1,0:T(8,128)}, f32[27,16,96]{2,1,0:T(8,128)}) custom-call(bf16[2,16,4,512]{3,2,1,0:T(4,128)(2,1)} %bitcast.12, bf16[13824,128]{1,0:T(8,128)(2,1)} %bitcast.8, f32[1,128]{1,0:T(1,128)} %bitcast.13, bf16[3456,384]{1,0:T(8,128)(2,1)} %bitcast.9, f32[384]{0:T(512)} %b2.1, bf16[16,2,4,1536]{3,2,1,0:T(4,128)(2,1)} %bitcast.11, ...), custom_call_target="tpu_custom_call" | custom-call | tf_op jit(solution)/shard_map/step/pallas_call | solution.py:419
  57.7 1.8 %copy.17 = f32[27,64,32]{1,2,0:T(8,128)} copy(f32[27,64,32]{1,2,0:T(8,128)} %bitcast.10) | data formatting | bytes 442368
  59.5 1.6 %copy.18 = f32[27,16,96]{2,1,0:T(8,128)} copy(f32[27,16,96]{2,1,0:T(8,128)} %get-tuple-element.9) | data formatting | bytes 331776

commit v2 on v1

--- a/solution.py
+++ b/solution.py
@@ -26,17 +26,20 @@
     vblk = values // ndp
     mblk = mid // nseq
     ndev = ndp * nseq
+    nz = nseq // 2
+    half = ndev // 2
     clip_lanes = nseq * n
 
     def kernel(tok, w1_hbm, b1, w2_hbm, b2, pix, marks, place_of, tperm, perm, colv, lanev,
                lanes_n, o1, o2,
                w1, w2, xbuf, xall, thalo, pxall, tfield, im1, hsend, hhalo, hfield, im2,
-               psend, phalo, csend, call_, htsend, htall, rsend, rall, gsend, gall, acc,
+               psend, phalo, csend, call_, htsend, htall, qsend, qrecv, rsend, rall, gsend, gall, acc,
                wsem, th_s, th_r, px_s, px_r, x_s, x_r, hh_s, hh_r, ph_s, ph_r,
-               c_s, c_r, ht_s, ht_r, r_s, r_r, g_s, g_r):
+               c_s, c_r, ht_s, ht_r, q_s, q_r, r_s, r_r, g_s, g_r):
         dp = lax.axis_index("dp")
         seq = lax.axis_index("seq")
         me = dp * nseq + seq
+        chip, core = seq // 2, lax.rem(seq, 2)
         nxt = lax.rem(seq + 1, nseq)
         prv = lax.rem(seq + nseq - 1, nseq)
 
@@ -108,12 +111,13 @@
                     remote(htsend, htall.at[d], ht_s.at[o], ht_r.at[d], d, seq))
 
         def r_copy(o):
-            s = lax.rem(seq + o, nseq)
-            return remote(rsend.at[s], rall.at[seq], r_s.at[o], r_r.at[seq], dp, s)
+            s = lax.rem(chip + o, nz)
+            return remote(rsend.at[s], rall.at[chip], r_s.at[o], r_r.at[chip], dp,
+                          s * 2 + core)
 
         def r_arrival(o):
-            s = lax.rem(seq + nseq - o, nseq)
-            return remote(rsend.at[s], rall.at[s], r_s.at[o], r_r.at[s], dp, s)
+            s = lax.rem(chip + nz - o, nz)
+            return remote(rsend.at[s], rall.at[s], r_s.at[o], r_r.at[s], dp, s * 2 + core)
 
         def g_copy(o):
             t = lax.rem(me + o, ndev)
@@ -125,21 +129,20 @@
             d = t // nseq
             return remote(gsend.at[d], gall.at[t], g_s.at[o], g_r.at[t], d, lax.rem(t, nseq))
 
-        def each(count, act):
+        def each(count, act, low=1):
             def body(o, c):
                 act(o)
                 return c
-            lax.fori_loop(1, count, body, 0)
-
-        def start_all(count, copy):
-            each(count, lambda o: copy(o).start())
+            lax.fori_loop(low, count, body, 0)
+
+        def start_all(count, copy, low=1):
+            each(count, lambda o: copy(o).start(), low)
 
         def finish(count, copy, arrival):
             each(count, lambda o: copy(o).wait_send())
             each(count, lambda o: arrival(o).wait_recv())
 
         start_all(nseq, px_copy)
-        start_all(ndev, x_copy)
         xall[me] = xbuf[seq]
         own = pltpu.make_async_copy(pix.at[pl.ds(seq * tf, tf)], pxall.at[seq], wsem.at[2])
         own.start()
@@ -210,6 +213,7 @@
 
         for c in hh:
             c.wait()
+        start_all(half, x_copy)
         before = hhalo[0].reshape(plane, mid).astype(F32) * first
         after = hhalo[1].reshape(plane, mid).astype(F32) * final
         place(hfield, 0, before, 1)
@@ -274,6 +278,7 @@
         for d in range(ndp):
             gsend[d] = grad_z[d * cblk:(d + 1) * cblk].astype(BF16)
         start_all(ndev, g_copy)
+        start_all(ndev, x_copy, half)
         gall[me] = gsend[dp]
 
         each(ndp, lambda o: [c.wait_send() for c in c_pair(o)])
@@ -296,12 +301,21 @@
             return carry
 
         lax.fori_loop(0, ndp, one_clip, 0)
-        for s in range(nseq):
+
+        def part(a, s):
+            return acc[pl.ds(pl.multiple_of(a * mid + s * mblk, 8), mblk)]
+
+        for s in range(nz):
             for a in range(3):
-                lo = a * mid + s * mblk
-                rsend[s, a] = acc[lo:lo + mblk].astype(BF16)
-        start_all(nseq, r_copy)
-        rall[seq] = rsend[seq]
+                qsend[s, a] = part(a, 2 * s + 1 - core).astype(BF16)
+        swap = remote(qsend, qrecv, q_s.at[0], q_r.at[0], dp, 2 * chip + 1 - core)
+        swap.start()
+        swap.wait()
+        for s in range(nz):
+            for a in range(3):
+                rsend[s, a] = (part(a, 2 * s + core) + qrecv[s, a].astype(F32)).astype(BF16)
+        start_all(nz, r_copy)
+        rall[chip] = rsend[chip]
 
         finish(ndev, x_copy, x_arrival)
         finish(ndev, g_copy, g_arrival)
@@ -344,9 +358,9 @@
 
         lax.fori_loop(0, ndp, one_first, 0)
 
-        finish(nseq, r_copy, r_arrival)
+        finish(nz, r_copy, r_arrival)
         total = rall[0].astype(F32)
-        for s in range(1, nseq):
+        for s in range(1, nz):
             total = total + rall[s].astype(F32)
         for a in range(3):
             for bc in range(9):
@@ -407,14 +421,16 @@
         pltpu.VMEM((ndp, 4, vblk, n), BF16),
         pltpu.VMEM((3 * mid, n), BF16),
         pltpu.VMEM((ndp, 3 * mid, n), BF16),
-        pltpu.VMEM((nseq, 3, mblk, 9 * vblk), BF16),
-        pltpu.VMEM((nseq, 3, mblk, 9 * vblk), BF16),
+        pltpu.VMEM((nseq // 2, 3, mblk, 9 * vblk), BF16),
+        pltpu.VMEM((nseq // 2, 3, mblk, 9 * vblk), BF16),
+        pltpu.VMEM((nseq // 2, 3, mblk, 9 * vblk), BF16),
+        pltpu.VMEM((nseq // 2, 3, mblk, 9 * vblk), BF16),
         pltpu.VMEM((ndp, cblk, n), BF16),
         pltpu.VMEM((ndev, cblk, n), BF16),
         pltpu.VMEM((3 * mid, 9 * vblk), F32),
         dma(3), dma(2), dma(2), dma(nseq), dma(nseq), dma(ndev), dma(ndev),
         dma(2), dma(2), dma(2), dma(2), dma(ndp), dma(ndp), dma(ndp), dma(ndp),
-        dma(nseq), dma(nseq), dma(ndev), dma(ndev),
+        dma(1), dma(1), dma(nseq // 2), dma(nseq // 2), dma(ndev), dma(ndev),
     ]
     first, second = pl.pallas_call(
         make_kernel(dims),

time: 61.4 us -> 57.3 us (0.933)
  the two profiles are of different devices: /device:TPU:9 before, /device:TPU:0 now
where the time goes in v2:
time: 57.3 us; the launch traced here: 57 us
  Pallas kernels  53 us (92%)
  local copies, waits for them, and re-layouts  3.44 us (6%)
  between operations  0.64 us (1%)
    pallas_call x1, Pallas kernels, per_device(): pl.pallas_call(make_kernel(dims), out_shape=(jax.ShapeDtypeStruct((27 * c...  53 us
    unnamed x2, local copies, waits for them, and re-layouts  3.44 us

profile of v2, /device:TPU:0, one launch (start us, length us, event | category | flops | bytes accessed | tf_op | source)
XLA Modules:
  0.0 57.0 jit_solution(10536396293494407184)
XLA Ops:
  0.6 53.0 %step.1 = (f32[864,64]{1,0:T(8,128)}, f32[27,16,96]{2,1,0:T(8,128)}) custom-call(bf16[2,16,4,512]{3,2,1,0:T(4,128)(2,1)} %bitcast.12, bf16[13824,128]{1,0:T(8,128)(2,1)} %bitcast.8, f32[1,128]{1,0:T(1,128)} %bitcast.13, bf16[3456,384]{1,0:T(8,128)(2,1)} %bitcast.9, f32[384]{0:T(512)} %b2.1, bf16[16,2,4,1536]{3,2,1,0:T(4,128)(2,1)} %bitcast.11, ...), custom_call_target="tpu_custom_call" | custom-call | tf_op jit(solution)/shard_map/step/pallas_call | solution.py:435
  53.6 1.8 %copy.17 = f32[27,64,32]{1,2,0:T(8,128)} copy(f32[27,64,32]{1,2,0:T(8,128)} %bitcast.10) | data formatting | bytes 442368
  55.4 1.6 %copy.18 = f32[27,16,96]{2,1,0:T(8,128)} copy(f32[27,16,96]{2,1,0:T(8,128)} %get-tuple-element.9) | data formatting | bytes 331776

commit v3 on v2

--- a/solution.py
+++ b/solution.py
@@ -142,7 +142,7 @@
             each(count, lambda o: copy(o).wait_send())
             each(count, lambda o: arrival(o).wait_recv())
 
-        start_all(nseq, px_copy)
+        start_all(nz, px_copy)
         xall[me] = xbuf[seq]
         own = pltpu.make_async_copy(pix.at[pl.ds(seq * tf, tf)], pxall.at[seq], wsem.at[2])
         own.start()
@@ -182,16 +182,21 @@
         edges(tfield)
         edges(hfield)
         place(tfield, 1, flat, tf)
+        def taps_first(a):
+            for bc in range(9):
+                k = a * 9 + bc
+                im1[:, k * width:(k + 1) * width] = (
+                    tfield[bc // 3, a:a + tf, bc % 3:bc % 3 + cols].reshape(n, width))
+            span = slice(a * 9 * width, (a + 1) * 9 * width)
+            return jnp.dot(im1[:, span], w1[span], preferred_element_type=F32)
+
+        cp1.wait()
+        z = taps_first(1) + b1[...]
         for c in th:
             c.wait()
         place(tfield, 0, ordered(thalo[0]) * first, 1)
         place(tfield, tf + 1, ordered(thalo[1]) * final, 1)
-        for k in range(27):
-            a, b, c = k // 9, k // 3 % 3, k % 3
-            im1[:, k * width:(k + 1) * width] = (
-                tfield[b, a:a + tf, c:c + cols].reshape(n, width))
-        cp1.wait()
-        z = jnp.dot(im1[...], w1[...], preferred_element_type=F32) + b1[...]
+        z = z + taps_first(0) + taps_first(2)
         th_ = jnp.tanh(GELU_ROOT * (z + GELU_CUBE * z * z * z))
         slope = 0.5 * (1.0 + th_) + 0.5 * z * (1.0 - th_ * th_) * GELU_ROOT * (
             1.0 + 3.0 * GELU_CUBE * z * z)
@@ -203,6 +208,36 @@
         hid_f = hid.astype(F32)
         place(hfield, 1, hid_f, tf)
 
+        start_all(nseq, px_copy, nz)
+
+        def taps_second(a):
+            for ij in range(4):
+                i, j = ij // 2, ij % 2
+                for bc in range(9):
+                    k = a * 9 + bc
+                    dh, dw = floor_half(i + bc // 3 - 1), floor_half(j + bc % 3 - 1)
+                    im2[ij * n:(ij + 1) * n, k * mid:(k + 1) * mid] = (
+                        hfield[dh + 1, a:a + tf, dw + 1:dw + 1 + cols].reshape(n, mid))
+            span = slice(a * 9 * mid, (a + 1) * 9 * mid)
+            return jnp.dot(im2[:, span], w2[span], preferred_element_type=F32)
+
+        cp2.wait()
+        predict = taps_second(1) + b2[...].reshape(1, values)
+        for c in hh:
+            c.wait()
+        start_all(half, x_copy)
+        before = hhalo[0].reshape(plane, mid).astype(F32) * first
+        after = hhalo[1].reshape(plane, mid).astype(F32) * final
+        time_line = jnp.concatenate([before, hid_f, after], axis=0)
+        for a in range(3):
+            htsend[a * mid:(a + 1) * mid] = (
+                time_line[a * plane:a * plane + n].T.astype(BF16))
+        each(ndp, lambda o: c_pair(o)[1].start())
+        htall[dp] = htsend[...]
+        place(hfield, 0, before, 1)
+        place(hfield, tf + 1, after, 1)
+        predict = predict + taps_second(0) + taps_second(2)
+
         own.wait()
         finish(nseq, px_copy, px_arrival)
         pix_rows = pxall[...].astype(F32).reshape(n, 4 * values).astype(BF16)
@@ -210,24 +245,6 @@
         center = px - jnp.mean(px, axis=-1, keepdims=True)
         spread = jnp.mean(center * center, axis=-1, keepdims=True)
         normed = center * lax.rsqrt(spread + 1e-06)
-
-        for c in hh:
-            c.wait()
-        start_all(half, x_copy)
-        before = hhalo[0].reshape(plane, mid).astype(F32) * first
-        after = hhalo[1].reshape(plane, mid).astype(F32) * final
-        place(hfield, 0, before, 1)
-        place(hfield, tf + 1, after, 1)
-
-        for ij in range(4):
-            i, j = ij // 2, ij % 2
-            for k in range(27):
-                a, b, c = k // 9, k // 3 % 3, k % 3
-                dh, dw = floor_half(i + b - 1), floor_half(j + c - 1)
-                im2[ij * n:(ij + 1) * n, k * mid:(k + 1) * mid] = (
-                    hfield[dh + 1, a:a + tf, dw + 1:dw + 1 + cols].reshape(n, mid))
-        cp2.wait()
-        predict = jnp.dot(im2[...], w2[...], preferred_element_type=F32) + b2[...].reshape(1, values)
         cots = []
         for ij in range(4):
             cot = (scale * (predict[ij * n:(ij + 1) * n]
@@ -236,13 +253,8 @@
             turned = cot.T
             for d in range(ndp):
                 csend[d, ij] = turned[d * vblk:(d + 1) * vblk].astype(BF16)
-        time_line = jnp.concatenate([before, hid_f, after], axis=0)
-        for a in range(3):
-            htsend[a * mid:(a + 1) * mid] = (
-                time_line[a * plane:a * plane + n].T.astype(BF16))
-        each(ndp, lambda o: [c.start() for c in c_pair(o)])
+        each(ndp, lambda o: c_pair(o)[0].start())
         call_[dp] = csend[dp]
-        htall[dp] = htsend[...]
 
         def pair_sums(low, high, shift):
             return (high + shift(low, 1), low + high, shift(high, -1) + low)

time: 57.3 us -> 55.7 us (0.972)
  Pallas kernels: 53 us -> 51.4 us
    pallas_call x1, Pallas kernels: 53 us -> 51.4 us  [per_device(): pl.pallas_call(make_kernel(dims), out_shape=(jax.ShapeDtypeStruct((27 * c...]
where the time goes in v3:
time: 55.7 us; the launch traced here: 55.5 us
  Pallas kernels  51.4 us (92%)
  local copies, waits for them, and re-layouts  3.44 us (6%)
  between operations  0.64 us (1%)
    pallas_call x1, Pallas kernels, per_device(): pl.pallas_call(make_kernel(dims), out_shape=(jax.ShapeDtypeStruct((27 * c...  51.4 us
    unnamed x2, local copies, waits for them, and re-layouts  3.44 us

profile of v3, /device:TPU:0, one launch (start us, length us, event | category | flops | bytes accessed | tf_op | source)
XLA Modules:
  0.0 55.5 jit_solution(1126553219383289898)
XLA Ops:
  0.6 51.4 %step.1 = (f32[864,64]{1,0:T(8,128)}, f32[27,16,96]{2,1,0:T(8,128)}) custom-call(bf16[2,16,4,512]{3,2,1,0:T(4,128)(2,1)} %bitcast.12, bf16[13824,128]{1,0:T(8,128)(2,1)} %bitcast.8, f32[1,128]{1,0:T(1,128)} %bitcast.13, bf16[3456,384]{1,0:T(8,128)(2,1)} %bitcast.9, f32[384]{0:T(512)} %b2.1, bf16[16,2,4,1536]{3,2,1,0:T(4,128)(2,1)} %bitcast.11, ...), custom_call_target="tpu_custom_call" | custom-call | tf_op jit(solution)/shard_map/step/pallas_call | solution.py:447
  52.1 1.8 %copy.17 = f32[27,64,32]{1,2,0:T(8,128)} copy(f32[27,64,32]{1,2,0:T(8,128)} %bitcast.10) | data formatting | bytes 442368
  53.9 1.6 %copy.18 = f32[27,16,96]{2,1,0:T(8,128)} copy(f32[27,16,96]{2,1,0:T(8,128)} %get-tuple-element.9) | data formatting | bytes 331776

commit v4 on v3

--- a/solution.py
+++ b/solution.py
@@ -27,7 +27,7 @@
     mblk = mid // nseq
     ndev = ndp * nseq
     nz = nseq // 2
-    half = ndev // 2
+    quarter = ndev // 4
     clip_lanes = nseq * n
 
     def kernel(tok, w1_hbm, b1, w2_hbm, b2, pix, marks, place_of, tperm, perm, colv, lanev,
@@ -143,6 +143,7 @@
             each(count, lambda o: arrival(o).wait_recv())
 
         start_all(nz, px_copy)
+        start_all(quarter, x_copy)
         xall[me] = xbuf[seq]
         own = pltpu.make_async_copy(pix.at[pl.ds(seq * tf, tf)], pxall.at[seq], wsem.at[2])
         own.start()
@@ -225,7 +226,7 @@
         predict = taps_second(1) + b2[...].reshape(1, values)
         for c in hh:
             c.wait()
-        start_all(half, x_copy)
+        start_all(3 * quarter, x_copy, quarter)
         before = hhalo[0].reshape(plane, mid).astype(F32) * first
         after = hhalo[1].reshape(plane, mid).astype(F32) * final
         time_line = jnp.concatenate([before, hid_f, after], axis=0)
@@ -290,7 +291,7 @@
         for d in range(ndp):
             gsend[d] = grad_z[d * cblk:(d + 1) * cblk].astype(BF16)
         start_all(ndev, g_copy)
-        start_all(ndev, x_copy, half)
+        start_all(ndev, x_copy, 3 * quarter)
         gall[me] = gsend[dp]
 
         each(ndp, lambda o: [c.wait_send() for c in c_pair(o)])

time: 55.7 us -> 51.8 us (0.930)
  Pallas kernels: 51.4 us -> 47.5 us
    pallas_call x1, Pallas kernels: 51.4 us -> 47.5 us  [per_device(): pl.pallas_call(make_kernel(dims), out_shape=(jax.ShapeDtypeStruct((27 * c...]
where the time goes in v4:
time: 51.8 us; the launch traced here: 51.6 us
  Pallas kernels  47.5 us (92%)
  local copies, waits for them, and re-layouts  3.44 us (7%)
  between operations  0.64 us (1%)
    pallas_call x1, Pallas kernels, per_device(): pl.pallas_call(make_kernel(dims), out_shape=(jax.ShapeDtypeStruct((27 * c...  47.5 us
    unnamed x2, local copies, waits for them, and re-layouts  3.44 us

profile of v4, /device:TPU:0, one launch (start us, length us, event | category | flops | bytes accessed | tf_op | source)
XLA Modules:
  0.0 51.6 jit_solution(7912916037784463973)
XLA Ops:
  0.6 47.5 %step.1 = (f32[864,64]{1,0:T(8,128)}, f32[27,16,96]{2,1,0:T(8,128)}) custom-call(bf16[2,16,4,512]{3,2,1,0:T(4,128)(2,1)} %bitcast.12, bf16[13824,128]{1,0:T(8,128)(2,1)} %bitcast.8, f32[1,128]{1,0:T(1,128)} %bitcast.13, bf16[3456,384]{1,0:T(8,128)(2,1)} %bitcast.9, f32[384]{0:T(512)} %b2.1, bf16[16,2,4,1536]{3,2,1,0:T(4,128)(2,1)} %bitcast.11, ...), custom_call_target="tpu_custom_call" | custom-call | tf_op jit(solution)/shard_map/step/pallas_call | solution.py:448
  48.1 1.8 %copy.17 = f32[27,64,32]{1,2,0:T(8,128)} copy(f32[27,64,32]{1,2,0:T(8,128)} %bitcast.10) | data formatting | bytes 442368
  49.9 1.6 %copy.18 = f32[27,16,96]{2,1,0:T(8,128)} copy(f32[27,16,96]{2,1,0:T(8,128)} %get-tuple-element.9) | data formatting | bytes 331776
